TPU v7x, 128 devices: a whole 4x4x4 slice. The times are simulated.
128 devices in a mesh: tm: 8 (over y, x_hi), agent: 16 (over z, x_lo, core).
Axes of the slice: x: 4 (x_hi: 2, x_lo: 2; x = x_hi * 2 + x_lo), y: 4, z: 4, core: 2. Of those that a mesh axis runs over, the one named last changes fastest.
Arguments:
- tokens: bfloat16 [32, 1024, 1024], P('tm', 'agent'), may hold values from -6 to 6
- conv_taps: float32 [5, 1024], replicated, may hold values from -3 to 3
- norm_first: float32 [1024], replicated, may hold values from 0.1 to 1.9
- norm_second: float32 [1024], replicated, may hold values from 0.1 to 1.9
- norm_third: float32 [1024], replicated, may hold values from 0.1 to 1.9
- w_in: bfloat16 [1024, 3072], replicated, may hold values from -0.1875 to 0.1875
- w_out: bfloat16 [3072, 1024], replicated, may hold values from -0.109375 to 0.109375
- w_query: bfloat16 [1024, 1024], replicated, may hold values from -16 to 16
- w_key: bfloat16 [1024, 1024], replicated, may hold values from -16 to 16
- w_value: bfloat16 [1024, 1024], replicated, may hold values from -0.1875 to 0.1875
- w_output: bfloat16 [1024, 1024], replicated, may hold values from -0.1875 to 0.1875
- agent_order: int32 [1024], P('agent'), may hold values from 0 to 1023, each once
- present_steps: int32 [1024], P('agent'), may hold values from 1 to 32
Outputs:
- result: bfloat16 [32, 1024, 1024], P('tm', 'agent')
Inputs may be any that keep to these rules, and one draw needn't show every extreme that they name: `agent_order`: each of 0 to 1023 appears once.
All inputs are finite; a program needn't handle non-finite values.
Results may differ from a plain program's by a relative error of at most 0.012.
Values may be sent and summed in bfloat16 or wider, within the bound.
A program may use at most 192 MiB of HBM per device.

v0:
```python
import jax
import jax.numpy as jnp
from jax import lax
from jax.sharding import PartitionSpec as P

HEADS = 16


EPS = 1e-05


def shifted(shard, axis, by):
    count = lax.axis_size(axis)
    pairs = [(i, i + by) for i in range(count) if 0 <= i + by < count]
    return lax.ppermute(shard, axis, pairs)


def normed_rows(rows, gain):
    values = rows.astype(jnp.float32)
    scale = lax.rsqrt(jnp.mean(values * values, axis=-1, keepdims=True) + EPS)
    return values * scale * gain


def make_absorb(query, own_order, steps, heads_here, project):
    step_count, agent_count, width = query.shape
    head_size = width // heads_here
    scale = head_size ** (-0.5)
    split_query = query.reshape(step_count, agent_count, heads_here, head_size)
    init = (
        jnp.full((step_count, heads_here, agent_count), -1e30, jnp.float32),
        jnp.zeros((step_count, heads_here, agent_count), jnp.float32),
        jnp.zeros((step_count, agent_count, heads_here, head_size), jnp.float32),
    )

    def absorb(carry, piece, start):
        best, total, summed = carry
        key_piece, value_piece, order_piece, present_piece = project(piece)
        count = key_piece.shape[1]
        key_piece = key_piece.reshape(step_count, count, heads_here, head_size)
        value_piece = value_piece.reshape(step_count, count, heads_here, head_size)
        scores = (
            jnp.einsum(
                "sahd,sbhd->shab", split_query, key_piece, preferred_element_type=jnp.float32
            )
            * scale
        )
        other_order = order_piece[0]
        earlier = other_order[None, None, :] < own_order[None, :, None]
        alive = steps[:, None, None] < present_piece[0][None, None, :]
        itself = other_order[None, None, :] == own_order[None, :, None]
        visible = (earlier & alive | itself)[:, None]
        masked = jnp.where(visible, scores, -1e30)
        fresh = jnp.maximum(best, jnp.max(masked, axis=-1))
        weights = jnp.where(visible, jnp.exp(masked - fresh[..., None]), 0.0).astype(jnp.bfloat16)
        total = jnp.sum(weights.astype(jnp.float32), axis=-1)
        part_sum = jnp.einsum(
            "shab,sbhd->sahd", weights, value_piece, preferred_element_type=jnp.float32
        )
        summed = part_sum
        return (fresh, total, summed)

    return (absorb, init)


def finish(carry, shape):
    best, total, summed = carry
    attended = summed / jnp.transpose(total, (0, 2, 1))[..., None]
    return attended.astype(jnp.bfloat16).reshape(shape)


def identity_piece(piece):
    return piece


def per_device(
    tokens,
    conv_taps,
    norm_first,
    norm_second,
    norm_third,
    w_in,
    w_out,
    w_query,
    w_key,
    w_value,
    w_output,
    agent_order,
    present_steps,
):
    step_count, agent_count, width = tokens.shape
    reach = conv_taps.shape[0] - 1
    earlier_steps = shifted(tokens, "tm", 1)
    extended = normed_rows(jnp.concatenate([earlier_steps, tokens], axis=0), norm_first)
    mixed = jnp.zeros((step_count, agent_count, width), jnp.float32)
    for lag in range(reach + 1):
        mixed = mixed + conv_taps[lag] * extended[reach - lag : reach - lag + step_count]
    first = (tokens.astype(jnp.float32) + mixed).astype(jnp.bfloat16)
    flat = first.reshape(step_count * agent_count, width)
    inner = normed_rows(flat, norm_second).astype(jnp.bfloat16)
    hidden = jax.nn.gelu(
        jnp.dot(inner, w_in, preferred_element_type=jnp.float32), approximate=False
    ).astype(jnp.bfloat16)
    second = (
        flat.astype(jnp.float32) + jnp.dot(hidden, w_out, preferred_element_type=jnp.float32)
    ).astype(jnp.bfloat16)
    attn_in = normed_rows(second, norm_third).astype(jnp.bfloat16)
    query = (
        jnp.dot(attn_in, w_query, preferred_element_type=jnp.float32)
        .astype(jnp.bfloat16)
        .reshape(step_count, agent_count, width)
    )
    order_rows = agent_order.reshape(1, agent_count)
    present_rows = present_steps.reshape(1, agent_count)
    keys = (
        jnp.dot(attn_in, w_key, preferred_element_type=jnp.float32)
        .astype(jnp.bfloat16)
        .reshape(step_count, agent_count, width)
    )
    values = (
        jnp.dot(attn_in, w_value, preferred_element_type=jnp.float32)
        .astype(jnp.bfloat16)
        .reshape(step_count, agent_count, width)
    )
    keys, values = (keys, values)
    query, keys, values = (
        lax.all_to_all(query, "tm", split_axis=2, concat_axis=0, tiled=True),
        lax.all_to_all(keys, "tm", split_axis=2, concat_axis=0, tiled=True),
        lax.all_to_all(values, "tm", split_axis=2, concat_axis=0, tiled=True),
    )
    steps = jnp.arange(query.shape[0], dtype=jnp.int32)
    heads_here = HEADS // lax.axis_size("tm")
    absorb, init = make_absorb(query, agent_order, steps, heads_here, identity_piece)
    carry = absorb(
        init,
        (
            lax.all_gather(keys, "agent", axis=1, tiled=True),
            lax.all_gather(values, "agent", axis=1, tiled=True),
            lax.all_gather(order_rows, "agent", axis=1, tiled=True),
            lax.all_gather(present_rows, "agent", axis=1, tiled=True),
        ),
        jnp.int32(0),
    )
    attended = finish(carry, query.shape)
    attended = lax.all_to_all(attended, "tm", split_axis=0, concat_axis=2, tiled=True)
    projected = jnp.dot(
        attended.reshape(step_count * agent_count, width),
        w_output,
        preferred_element_type=jnp.float32,
    )
    result = second.astype(jnp.float32) + projected
    return result.astype(jnp.bfloat16).reshape(step_count, agent_count, width)


def solution(mesh):
    in_specs = (
        P("tm", "agent", None),
        P(),
        P(),
        P(),
        P(),
        P(),
        P(),
        P(),
        P(),
        P(),
        P(),
        P("agent"),
        P("agent"),
    )
    out_specs = P("tm", "agent", None)
    return jax.shard_map(
        per_device, mesh=mesh, in_specs=in_specs, out_specs=out_specs, check_vma=False
    )
```

profile of v0, /device:TPU:1, one launch (start us, length us, event | category | flops | bytes accessed | tf_op | source)
XLA Modules:
  0.0 234.9 jit_solution(14129081017646608805)
XLA Ops:
  6.5 5.8 %collective-permute-start = (bf16[4,64,1024]{2,1,0:T(8,128)(2,1)}, bf16[4,64,1024]{2,1,0:T(8,128)(2,1)S(1)}, u32[]{:S(2)}, u32[]{:S(2)}) collective-permute-start(bf16[4,64,1024]{2,1,0:T(8,128)(2,1)} %param.13), channel_id=1, source_target_pairs={{0,16},{16,32},{32,48},{48,64},{64,80},{80,96},{96,112},{1,17},{17... | collective-permute-start | bytes 1572872 | tf_op jit(solution)/shard_map/ppermute | solution.py:15
  12.3 1.0 fusion.102
  13.3 9.9 %collective-permute-done = bf16[4,64,1024]{2,1,0:T(8,128)(2,1)S(1)} collective-permute-done((bf16[4,64,1024]{2,1,0:T(8,128)(2,1)}, bf16[4,64,1024]{2,1,0:T(8,128)(2,1)S(1)}, u32[]{:S(2)}, u32[]{:S(2)}) %collective-permute-start) | collective-permute-done | bytes 524320 | tf_op jit(solution)/shard_map/ppermute | solution.py:15
  23.2 1.3 fusion.11
  24.5 1.3 fusion.12
  26.8 15.0 %fusion.53 = (f32[256]{0:T(256)S(1)}, bf16[256,1024]{1,0:T(8,128)(2,1)}) fusion(bf16[3072,1024]{1,0:T(8,128)(2,1)} %param.19, bf16[256,1024]{1,0:T(8,128)(2,1)S(1)} %fusion.63, bf16[1024,3072]{1,0:T(8,128)(2,1)} %param.18, bf16[256,1024]{1,0:T(8,128)(2,1)S(1)} %bitcast.69), kind=kOutput, calls=%fused_computation.70 | convolution fusion | flops 3273916160 | bytes 14156800 | tf_op jit(solution)/shard_map/dot_general | solution.py:104
  41.8 1.8 convolution_convert_fusion
  43.6 0.9 copy.31
  45.3 16.8 %all_to_all.66 = bf16[8,2,16384]{2,1,0:T(2,128)(2,1)S(1)} all-to-all(bf16[8,2,16384]{2,1,0:T(2,128)(2,1)S(1)} %reshape.197), channel_id=1, replica_groups=mesh['tm'=8,'agent'=16] {'tm'}, dimensions={0} | all-to-all | bytes 1048576 | tf_op jit(solution)/shard_map/all_to_all | solution.py:127
  62.7 1.4 copy.32
  64.2 2.3 convolution_convert_fusion.2
  66.5 0.7 copy.25
  68.0 12.1 %all_to_all.67 = bf16[8,2,16384]{2,1,0:T(2,128)(2,1)S(1)} all-to-all(bf16[8,2,16384]{2,1,0:T(2,128)(2,1)S(1)} %reshape.195), channel_id=1, replica_groups=mesh['tm'=8,'agent'=16] {'tm'}, dimensions={0} | all-to-all | bytes 1048576 | tf_op jit(solution)/shard_map/all_to_all | solution.py:128
  80.8 1.3 copy.26
  84.0 20.6 %all-reduce.2 = (s32[1024]{0:T(1024)S(1)}, s32[1024]{0:T(1024)S(1)}) all-reduce(s32[1024]{0:T(1024)S(1)} %dynamic-update-slice, s32[1024]{0:T(1024)S(1)} %dynamic-update-slice.1), channel_id=2, replica_groups=mesh['tm'=8,'agent'=16] {'agent'}, use_global_device_ids=true, to_apply=%add | all-reduce | flops 2048 | bytes 16384
  104.8 2.4 %convolution_convert_fusion.1 = bf16[256,1024]{1,0:T(8,128)(2,1)S(1)} fusion(bf16[1024,1024]{1,0:T(8,128)(2,1)} %param.20, bf16[256,1024]{1,0:T(8,128)(2,1)S(1)} %copy-done.8, f32[1024]{0:T(1024)S(1)} %copy-done.5, f32[256]{0:T(256)S(1)} %add_rsqrt_fusion.2), kind=kOutput, calls=%fused_computation.67 | convolution fusion | flops 538181632 | bytes 3150848 | tf_op jit(solution)/shard_map/dot_general | solution.py:108
  107.8 1.5 reshape.199
  109.3 4.4 %all-to-all-start.1 = ((bf16[8,2,16384]{2,1,0:T(2,128)(2,1)}), bf16[8,2,16384]{2,1,0:T(2,128)(2,1)}, u32[]{:S(2)}, u32[]{:S(2)}) async-start(bf16[8,2,16384]{2,1,0:T(2,128)(2,1)} %reshape.199), calls=%async_computation.1 | async-start | bytes 1048576 | tf_op jit(solution)/shard_map/all_to_all | solution.py:126
  113.7 1.4 and_or_fusion
  115.1 11.6 %all-to-all-done.1 = bf16[8,2,16384]{2,1,0:T(2,128)(2,1)} async-done(((bf16[8,2,16384]{2,1,0:T(2,128)(2,1)}), bf16[8,2,16384]{2,1,0:T(2,128)(2,1)}, u32[]{:S(2)}, u32[]{:S(2)}) %all-to-all-start.1) | async-done | bytes 524320 | tf_op jit(solution)/shard_map/all_to_all | solution.py:126
  126.8 2.7 %reshape.200 = bf16[1024,4,64]{2,1,0:T(4,128)(2,1)S(1)} reshape(bf16[8,2,16384]{2,1,0:T(2,128)(2,1)} %all-to-all-done.1) | data formatting | bytes 1048576
  129.5 1.2 copy.38
  130.7 2.4 %reshape.174 = bf16[32,64,2,64]{3,2,1,0:T(2,128)(2,1)S(1)} reshape(bf16[8,4,64,128]{3,2,1,0:T(8,128)(2,1)} %bitcast.70) | data formatting | bytes 1048576 | tf_op jit(solution)/shard_map/reshape | solution.py:28
  133.2 12.2 %copy.33 = bf16[32,1024,128]{1,2,0:T(8,128)(2,1)} copy(bf16[32,1024,128]{2,0,1:T(8,128)(2,1)} %all-gather.7.cloned.1.call-done) | data formatting | bytes 16777216 | tf_op jit(solution)/shard_map/all_gather | solution.py:136
  145.4 10.4 %fusion = (f32[32,2,64]{2,1,0:T(2,128)S(1)}, f32[32,2,64,1024]{3,2,1,0:T(8,128)}) fusion(pred[32,64,1024]{2,1,0:T(8,128)(4,1)S(1)} %and_or_fusion, bf16[32,1024,2,64]{1,3,2,0:T(8,128)(2,1)} %bitcast.61, bf16[32,64,2,64]{3,2,1,0:T(2,128)(2,1)S(1)} %reshape.174), kind=kOutput, calls=%fused_computation.3 | convolution fusion | flops 549449728 | bytes 27803648 | tf_op jit(solution)/shard_map/sahd,sbhd->shab/dot_general | solution.py:42
  155.8 9.0 %convert_reduce_fusion = f32[32,2,64]{2,1,0:T(2,128)S(1)} fusion(f32[32,2,64]{2,1,0:T(2,128)S(1)} %broadcast_maximum_fusion, f32[32,2,64,1024]{3,2,1,0:T(8,128)} %get-tuple-element.19, pred[32,64,1024]{2,1,0:T(8,128)(4,1)S(1)} %and_or_fusion), kind=kLoop, calls=%fused_computation | loop fusion | flops 29356032 | bytes 18907136 | tf_op jit(solution)/shard_map/reduce_sum | solution.py:55
  164.8 17.0 %all-gather.5.cloned.1.call-done = bf16[32,1024,128]{2,0,1:T(8,128)(2,1)} async-done(((bf16[32,64,128]{2,0,1:T(8,128)(2,1)}), bf16[32,1024,128]{2,0,1:T(8,128)(2,1)}) %all-gather.5.cloned.1.call-update) | async-done | bytes 8388624 | tf_op jit(solution)/shard_map/all_gather | solution.py:137
  181.8 12.2 %copy.27 = bf16[32,1024,128]{1,2,0:T(8,128)(2,1)} copy(bf16[32,1024,128]{2,0,1:T(8,128)(2,1)} %all-gather.5.cloned.1.call-done) | data formatting | bytes 16777216 | tf_op jit(solution)/shard_map/all_gather | solution.py:137
  194.0 11.7 %fusion.13 = bf16[32,64,2,64]{1,3,2,0:T(8,128)(2,1)} fusion(bf16[32,1024,2,64]{1,3,2,0:T(8,128)(2,1)} %bitcast.62, f32[32,64,2]{1,2,0:T(2,128)S(1)} %bitcast.79, f32[32,2,64,1024]{3,2,1,0:T(8,128)} %get-tuple-element.19, f32[32,2,64]{2,1,0:T(2,128)S(1)} %broadcast_maximum_fusion, pred[32,64,1024]{2,1,0:T(8,128)(4,1)S(1)} %and_or_fusion), kind=kOutput, calls=%fused_computation.29 | convolution fusion | flops 558366720 | bytes 27820032 | tf_op jit(solution)/shard_map/shab,sbhd->sahd/dot_general | solution.py:56
  205.7 1.7 copy.35
  207.5 17.1 %all_to_all.68 = bf16[32,64,128]{2,1,0:T(8,128)(2,1)S(1)} all-to-all(bf16[32,64,128]{2,1,0:T(8,128)(2,1)S(1)} %copy.35), channel_id=1, replica_groups=mesh['tm'=8,'agent'=16] {'tm'}, dimensions={0} | all-to-all | bytes 1048576 | tf_op jit(solution)/shard_map/all_to_all | solution.py:144
  224.9 3.1 %fusion.49 = bf16[256,1024]{1,0:T(8,128)(2,1)} fusion(bf16[1024,1024]{1,0:T(8,128)(2,1)} %param.23, bf16[256,1024]{1,0:T(8,128)(2,1)S(1)} %copy-done.9, bf16[32,8,8,128]{3,2,1,0:T(8,128)(2,1)S(1)} %bitcast.78), kind=kOutput, calls=%fused_computation.65 | convolution fusion | flops 537657344 | bytes 3670016 | tf_op jit(solution)/shard_map/dot_general | solution.py:145
  (45 shorter events, 6.1 us)
Async XLA Ops:
  6.5 35.3 %copy-start = (bf16[1024,1024]{1,0:T(8,128)(2,1)S(1)}, bf16[1024,1024]{1,0:T(8,128)(2,1)}, u32[]{:S(2)}) copy-start(bf16[1024,1024]{1,0:T(8,128)(2,1)} %param.21) | copy-start | bytes 6291460
  6.5 19.3 %copy-start.2 = (bf16[4,64,1024]{2,1,0:T(8,128)(2,1)S(1)}, bf16[4,64,1024]{2,1,0:T(8,128)(2,1)}, u32[]{:S(2)}) copy-start(bf16[4,64,1024]{2,1,0:T(8,128)(2,1)} %param.13) | copy-start | bytes 1572868
  6.5 126.7 %all-gather.7.cloned.1.call-start = ((), (), s32[]{:S(2)}) async-start(), calls=%async_computation.5 | async-start | bytes 8912896 | tf_op jit(solution)/shard_map/all_gather | solution.py:136
  6.5 16.6 %collective-permute-start = (bf16[4,64,1024]{2,1,0:T(8,128)(2,1)}, bf16[4,64,1024]{2,1,0:T(8,128)(2,1)S(1)}, u32[]{:S(2)}, u32[]{:S(2)}) collective-permute-start(bf16[4,64,1024]{2,1,0:T(8,128)(2,1)} %param.13), channel_id=1, source_target_pairs={{0,16},{16,32},{32,48},{48,64},{64,80},{80,96},{96,112},{1,17},{17... | collective-permute-start | bytes 1572872 | tf_op jit(solution)/shard_map/ppermute | solution.py:15
  25.8 0.7 copy-start.3
  26.8 15.1 %copy-start.5 = (f32[1024]{0:T(1024)S(1)}, f32[1024]{0:T(1024)}, u32[]{:S(2)}) copy-start(f32[1024]{0:T(1024)} %param.17) | copy-start | bytes 12292
  44.5 19.6 %copy-start.8 = (bf16[256,1024]{1,0:T(8,128)(2,1)S(1)}, bf16[256,1024]{1,0:T(8,128)(2,1)}, u32[]{:S(2)}) copy-start(bf16[256,1024]{1,0:T(8,128)(2,1)} %get-tuple-element.17) | copy-start | bytes 1572868
  64.1 117.7 %all-gather.5.cloned.1.call-start = ((), (), s32[]{:S(2)}) async-start(), calls=%async_computation.4 | async-start | bytes 8912896 | tf_op jit(solution)/shard_map/all_gather | solution.py:137
  67.3 14.9 %copy-start.7 = (u32[128]{0:T(128)S(1)}, u32[128]{0:T(128)}, u32[]{:S(2)}) copy-start(u32[128]{0:T(128)} %constant.80) | copy-start | bytes 1540
  67.3 16.3 %copy-start.4 = (s32[64]{0:T(128)S(1)}, s32[64]{0:T(128)}, u32[]{:S(2)}) copy-start(s32[64]{0:T(128)} %param.24) | copy-start | bytes 772
  67.3 16.5 %copy-start.6 = (s32[64]{0:T(128)S(1)}, s32[64]{0:T(128)}, u32[]{:S(2)}) copy-start(s32[64]{0:T(128)} %param.25) | copy-start | bytes 772
  109.3 17.4 %all-to-all-start.1 = ((bf16[8,2,16384]{2,1,0:T(2,128)(2,1)}), bf16[8,2,16384]{2,1,0:T(2,128)(2,1)}, u32[]{:S(2)}, u32[]{:S(2)}) async-start(bf16[8,2,16384]{2,1,0:T(2,128)(2,1)} %reshape.199), calls=%async_computation.1 | async-start | bytes 1048576 | tf_op jit(solution)/shard_map/all_to_all | solution.py:126
  205.7 19.2 %copy-start.9 = (bf16[256,1024]{1,0:T(8,128)(2,1)S(1)}, bf16[256,1024]{1,0:T(8,128)(2,1)}, u32[]{:S(2)}) copy-start(bf16[256,1024]{1,0:T(8,128)(2,1)} %get-tuple-element.17) | copy-start | bytes 1572868
  205.7 22.3 %copy-start.1 = (bf16[1024,1024]{1,0:T(8,128)(2,1)S(1)}, bf16[1024,1024]{1,0:T(8,128)(2,1)}, u32[]{:S(2)}) copy-start(bf16[1024,1024]{1,0:T(8,128)(2,1)} %param.21) | copy-start | bytes 6291460
Sparse Core Ops, SparseCore 0:
  64.2 55.9 all-gather.6
  122.0 59.8 all-gather.4
where the time goes:
time: 236 us; the launch traced here: 235 us
  blocking collectives  66.6 us (28%)
  matrix products  46.7 us (20%)
  local copies, waits for them, and re-layouts  44.3 us (19%)
  waiting for transfers between devices  38.6 us (16%)
  between operations  14.4 us (6%)
  other arithmetic  14.1 us (6%)
  starting transfers between devices  10.2 us (4%)
    unnamed x1, blocking collectives  20.6 us
    all_to_all x1, blocking collectives, per_device(): lax.all_to_all(attended, 'tm', split_axis=0, concat_axis=2, tiled=True)  17.1 us
    all_gather x1, waiting for transfers between devices, per_device(): lax.all_gather(values, 'agent', axis=1, tiled=True)  17 us
    all_to_all x1, blocking collectives, per_device(): lax.all_to_all(keys, 'tm', split_axis=2, concat_axis=0, tiled=True)  16.8 us
    dot_general x1, matrix products, per_device(): jnp.dot(hidden, w_out, preferred_element_type=jnp.float32)  15 us
    all_gather x1, local copies, waits for them, and re-layouts, per_device(): lax.all_gather(keys, 'agent', axis=1, tiled=True)  12.2 us
    all_gather x1, local copies, waits for them, and re-layouts, per_device(): lax.all_gather(values, 'agent', axis=1, tiled=True)  12.2 us
    all_to_all x1, blocking collectives, per_device(): lax.all_to_all(values, 'tm', split_axis=2, concat_axis=0, tiled=True)  12.1 us
  transfers between devices with their start and end apart: 4, of which 3 were waited for; matrix products, arithmetic and copies ran while one was open for 22% of the time, Pallas kernels for 0%

commit v1 on v0

v1 whole, which is shorter than its diff:
```python
import functools

import jax
import jax.numpy as jnp
from jax import lax
from jax.experimental import pallas as pl
from jax.experimental.pallas import tpu as pltpu
from jax.sharding import PartitionSpec as P

EPS = 1e-05
HEADS = 16
MESH = pl.DeviceIdType.MESH
F32, BF16 = jnp.float32, jnp.bfloat16
GROUP = 16
LAYERS = 4
ROWS = 64
WIDTH = 1024
HIDDEN = 3072
COLS = 256
FF_TILE = 512
BLOCKS = ((0, 1, 2, 3),)


def remote(src, dst, send, recv, tm, agent):
    return pltpu.make_async_remote_copy(
        src_ref=src,
        dst_ref=dst,
        send_sem=send,
        recv_sem=recv,
        device_id=(tm, agent),
        device_id_type=MESH,
    )


def normed(rows, gain):
    scale = lax.rsqrt(jnp.mean(rows * rows, axis=-1, keepdims=True) + EPS)
    return rows * scale * gain


def block_kernel(
    tokens,
    taps,
    gain_first,
    gain_second,
    gain_third,
    w_in,
    w_out,
    w_query,
    w_key,
    w_value,
    w_output,
    info_own,
    result,
    win_v,
    wout_v,
    wqkv_v,
    wo_v,
    tok_v,
    prev_v,
    norm_v,
    hid_v,
    second_v,
    mine_v,
    gath_v,
    query_v,
    key_v,
    value_v,
    att_v,
    back_v,
    info_v,
    okey_v,
    oquery_v,
    local_sem,
    shift_send,
    shift_recv,
    info_send,
    info_recv,
    ex_send,
    ex_recv,
    rel_send,
    rel_recv,
    ret_send,
    ret_recv,
):
    tm, me = lax.axis_index("tm"), lax.axis_index("agent")
    n_tm = lax.axis_size("tm")
    z, x, core = me // 4, lax.rem(me // 2, 2), lax.rem(me, 2)
    group = lax.rem(me, 4)
    sibling = me + 1 - 2 * core
    across = me + 2 - 4 * x
    after, before = lax.rem(tm + 1, n_tm), lax.rem(tm + n_tm - 1, n_tm)

    cols = pl.ds(pl.multiple_of(group * COLS, COLS), COLS)
    loads = [
        pltpu.make_async_copy(tokens, tok_v, local_sem.at[0]),
        pltpu.make_async_copy(w_in, win_v, local_sem.at[1]),
        pltpu.make_async_copy(w_out, wout_v, local_sem.at[2]),
        pltpu.make_async_copy(w_query.at[:, cols], wqkv_v.at[0], local_sem.at[3]),
        pltpu.make_async_copy(w_key.at[:, cols], wqkv_v.at[1], local_sem.at[4]),
        pltpu.make_async_copy(w_value.at[:, cols], wqkv_v.at[2], local_sem.at[5]),
        pltpu.make_async_copy(w_output, wo_v, local_sem.at[6]),
    ]
    for load in loads:
        load.start()

    barrier = pltpu.get_barrier_semaphore()

    def greet(d, carry):
        pl.semaphore_signal(
            barrier, inc=1, device_id=(tm, lax.rem(me + d, GROUP)), device_id_type=MESH
        )
        return carry

    pl.semaphore_signal(barrier, inc=1, device_id=(before, me), device_id_type=MESH)
    pl.semaphore_signal(barrier, inc=1, device_id=(after, me), device_id_type=MESH)
    lax.fori_loop(1, GROUP, greet, 0)
    pl.semaphore_wait(barrier, GROUP + 1)

    def shift(step):
        return remote(
            tokens.at[step],
            prev_v.at[step],
            shift_send.at[step],
            shift_recv.at[step],
            after,
            me,
        )

    order = (3, 2, 1, 0)

    @pl.when(tm < n_tm - 1)
    def _():
        for step in order:
            shift(step).start()

    @pl.when(tm == 0)
    def _():
        prev_v[...] = jnp.zeros_like(prev_v)

    def info_copy(slot, peer):
        return remote(
            info_own, info_v.at[slot], info_send.at[peer], info_recv.at[slot], tm, peer
        )

    def tell(d, carry):
        info_copy(me, lax.rem(me + d, GROUP)).start()
        return carry

    own_info = pltpu.make_async_copy(info_own, info_v.at[me], local_sem.at[7])
    own_info.start()
    lax.fori_loop(1, GROUP, tell, 0)

    gain1, gain2, gain3 = gain_first[...], gain_second[...], gain_third[...]
    loads[0].wait()
    for step in range(4):
        norm_v[4 + step] = normed(tok_v[step].astype(F32), gain1)
    arrived = set()
    local_pieces = []
    for number, block in enumerate(BLOCKS):
        for step in order:
            if step >= min(block) and step not in arrived:
                arrived.add(step)

                @pl.when(tm > 0)
                def _(step=step):
                    shift(step).wait_recv()

                norm_v[step] = normed(prev_v[step].astype(F32), gain1)
        rows = pl.ds(min(block) * ROWS, len(block) * ROWS)
        firsts = []
        for step in block:
            mixed = taps[0:1, :] * norm_v[step + 4]
            for lag in range(1, 5):
                mixed = mixed + taps[lag : lag + 1, :] * norm_v[step + 4 - lag]
            firsts.append((tok_v[step].astype(F32) + mixed).astype(BF16))
        first = jnp.concatenate(firsts, axis=0)
        second_v[rows, :] = first
        inner = normed(first.astype(F32), gain2).astype(BF16)
        if number == 0:
            loads[1].wait()
        for tile in range(0, HIDDEN, FF_TILE):
            pre = jnp.dot(inner, win_v[:, tile : tile + FF_TILE], preferred_element_type=F32)
            act = 0.5 * pre * (1.0 + lax.erf(pre * 0.7071067811865476))
            hid_v[rows, tile : tile + FF_TILE] = act.astype(BF16)
        if number == 0:
            loads[2].wait()
        ffn = jnp.dot(hid_v[rows, :], wout_v[...], preferred_element_type=F32)
        second = (second_v[rows, :].astype(F32) + ffn).astype(BF16)
        second_v[rows, :] = second
        attn_in = normed(second.astype(F32), gain3).astype(BF16)
        for spot, step in enumerate(block):
            mine_v[step] = attn_in[spot * ROWS : (spot + 1) * ROWS]

        for step in block:
            far = remote(
                mine_v.at[step],
                gath_v.at[me],
                ex_send.at[step * 2 + 1],
                ex_recv.at[me],
                tm,
                step * 4 + 2 * (1 - x) + core,
            )
            far.start()
            near = remote(
                mine_v.at[step],
                gath_v.at[me],
                ex_send.at[step * 2],
                ex_recv.at[me],
                tm,
                step * 4 + 2 * x + core,
            )

            @pl.when(z != step)
            def _(near=near):
                near.start()

            @pl.when(z == step)
            def _(step=step):
                pltpu.make_async_copy(
                    mine_v.at[step], gath_v.at[me], local_sem.at[8]
                ).start()
                remote(
                    mine_v.at[step],
                    gath_v.at[me],
                    rel_send.at[me],
                    rel_recv.at[me],
                    tm,
                    sibling,
                ).start()

    def arrive(slot, recv):
        remote(mine_v.at[0], gath_v.at[slot], ex_send.at[0], recv.at[slot], tm, me).wait_recv()

    def forward(slot):
        return remote(
            gath_v.at[slot],
            gath_v.at[slot],
            rel_send.at[slot],
            rel_recv.at[slot],
            tm,
            sibling,
        )

    own_info.wait()

    def heard(d, carry):
        peer = lax.rem(me + d, GROUP)
        info_copy(peer, peer).wait_recv()
        return carry

    lax.fori_loop(1, GROUP, heard, 0)
    now = tm * LAYERS + z
    low = lax.broadcasted_iota(jnp.int32, (1, 128), 1) < ROWS
    eye = lax.broadcasted_iota(jnp.int32, (128, 128), 0) == lax.broadcasted_iota(
        jnp.int32, (128, 128), 1
    )
    for pair in range(GROUP // 2):
        left, right = info_v[2 * pair], info_v[2 * pair + 1]
        place = jnp.where(low, left[0:1], right[0:1])
        until = jnp.where(low, left[1:2], right[1:2])
        place_f = place.astype(F32)
        span = slice(pair * 128, pair * 128 + 128)
        okey_v[0:1, span] = jnp.where(now < until, place_f, 1e9)
        oquery_v[span, :] = jnp.sum(
            jnp.where(eye, jnp.broadcast_to(place_f, (128, 128)), 0.0), axis=1, keepdims=True
        )

    for load in loads[3:6]:
        load.wait()
    lane = lax.broadcasted_iota(jnp.int32, (COLS, 128), 1) < 64

    def project(layer):
        rows = pl.ds(pl.multiple_of(layer * COLS, COLS), COLS)
        source = gath_v[pl.ds(layer * 4, 4)].reshape(COLS, WIDTH)
        query = jnp.dot(source, wqkv_v[0], preferred_element_type=F32) * 0.125
        key = jnp.dot(source, wqkv_v[1], preferred_element_type=F32)
        value = jnp.dot(source, wqkv_v[2], preferred_element_type=F32)
        for pair in range(2):
            span = slice(pair * 128, pair * 128 + 128)
            query_v[pair, rows, :] = query[:, span].astype(BF16)
            key_v[2 * pair, rows, :] = jnp.where(lane, key[:, span], 0.0).astype(BF16)
            key_v[2 * pair + 1, rows, :] = jnp.where(lane, 0.0, key[:, span]).astype(BF16)
            value_v[2 * pair, rows, :] = jnp.where(lane, value[:, span], 1.0).astype(BF16)
            value_v[2 * pair + 1, rows, :] = jnp.where(lane, 1.0, value[:, span]).astype(BF16)

    turns = (0, 1, 3, 2)

    def slots(turn):
        base = lax.rem(z + turn, LAYERS) * 4
        return base + 2 * x + core, base + 2 * (1 - x) + core

    def from_sibling(turn):
        for slot in slots(turn):
            arrive(slot + 1 - 2 * core, rel_recv)

    for index, turn in enumerate(turns):
        near, far = slots(turn)
        if turn:
            arrive(near, ex_recv)
            forward(near).start()
        arrive(far, ex_recv)
        forward(far).start()
        if turn == 0:
            pltpu.make_async_copy(mine_v.at[0], gath_v.at[me], local_sem.at[8]).wait()
        if index:
            from_sibling(turns[index - 1])
            project(lax.rem(z + turns[index - 1], LAYERS))
    from_sibling(turns[-1])
    project(lax.rem(z + turns[-1], LAYERS))

    home_cols = pl.ds(pl.multiple_of(group * COLS, COLS), COLS)

    def give(home):
        return remote(
            att_v.at[pl.ds(pl.multiple_of(home * ROWS, ROWS), ROWS), :],
            back_v.at[z, :, home_cols],
            ret_send.at[home],
            ret_recv.at[me],
            tm,
            home,
        )

    half = lax.broadcasted_iota(jnp.int32, (COLS, 128), 1) < 64

    def attend(index, carry):
        layer = lax.rem(z + 3 - index, LAYERS)
        start = pl.multiple_of(layer * COLS, COLS)
        rows = pl.ds(start, COLS)
        row = lax.broadcasted_iota(jnp.int32, (COLS, GROUP * ROWS), 0) + start
        column = lax.broadcasted_iota(jnp.int32, (COLS, GROUP * ROWS), 1)
        visible = (okey_v[0:1, :] < oquery_v[rows, :]) | (row == column)
        bias = jnp.where(visible, 0.0, -1e30)
        for pair in range(2):
            query = query_v[pair, rows, :]
            parts = []
            for head in (2 * pair, 2 * pair + 1):
                scores = lax.dot_general(
                    query,
                    key_v[head],
                    (((1,), (1,)), ((), ())),
                    preferred_element_type=F32,
                )
                scores = scores + bias
                top = jnp.max(scores, axis=-1, keepdims=True)
                weights = jnp.exp(scores - top).astype(BF16)
                parts.append(jnp.dot(weights, value_v[head], preferred_element_type=F32))
            summed = jnp.where(half, parts[0], parts[1])
            total = pltpu.roll(jnp.where(half, parts[1], parts[0]), 64, 1)
            att_v[rows, pair * 128 : pair * 128 + 128] = (summed / total).astype(BF16)
        for peer in range(4):
            home = layer * 4 + peer

            @pl.when(home != me)
            def _(home=home):
                give(home).start()

            @pl.when(home == me)
            def _(home=home):
                pltpu.make_async_copy(
                    att_v.at[pl.ds(pl.multiple_of(home * ROWS, ROWS), ROWS), :],
                    back_v.at[z, :, home_cols],
                    local_sem.at[9],
                ).start()

        return carry

    lax.fori_loop(0, LAYERS, attend, 0)

    def home_recv(d, carry):
        peer = lax.rem(me + d, GROUP)
        remote(
            att_v.at[pl.ds(0, ROWS), :],
            back_v.at[peer // 4, :, pl.ds(pl.multiple_of(lax.rem(peer, 4) * COLS, COLS), COLS)],
            ret_send.at[peer],
            ret_recv.at[peer],
            tm,
            peer,
        ).wait_recv()
        return carry

    pltpu.make_async_copy(
        att_v.at[pl.ds(0, ROWS), :], back_v.at[z, :, home_cols], local_sem.at[9]
    ).wait()
    lax.fori_loop(1, GROUP, home_recv, 0)
    loads[6].wait()
    projected = jnp.dot(
        back_v[...].reshape(4 * ROWS, WIDTH), wo_v[...], preferred_element_type=F32
    )
    result[...] = (
        (second_v[...].astype(F32) + projected).astype(BF16).reshape(4, ROWS, WIDTH)
    )

    @pl.when(tm < n_tm - 1)
    def _():
        for step in order:
            shift(step).wait_send()

    def drained(d, carry):
        peer = lax.rem(me + d, GROUP)
        info_copy(me, peer).wait_send()
        give(peer).wait_send()
        return carry

    lax.fori_loop(1, GROUP, drained, 0)
    for step in range(4):
        sent = remote(
            mine_v.at[step], gath_v.at[me], ex_send.at[step * 2 + 1], ex_recv.at[me], tm, across
        )
        sent.wait_send()
        sent = remote(
            mine_v.at[step], gath_v.at[me], ex_send.at[step * 2], ex_recv.at[me], tm, across
        )

        @pl.when(z != step)
        def _(sent=sent):
            sent.wait_send()

    for turn in turns:
        for slot in slots(turn):
            forward(slot).wait_send()


def per_device(
    tokens,
    conv_taps,
    norm_first,
    norm_second,
    norm_third,
    w_in,
    w_out,
    w_query,
    w_key,
    w_value,
    w_output,
    agent_order,
    present_steps,
):
    places = jnp.concatenate([agent_order, agent_order])
    untils = jnp.concatenate([present_steps, present_steps])
    info = jnp.stack([places, untils] * 4)
    vmem, hbm = pl.BlockSpec(memory_space=pltpu.VMEM), pl.BlockSpec(memory_space=pl.ANY)
    dma = pltpu.SemaphoreType.DMA
    everyone = GROUP * ROWS
    return pl.pallas_call(
        block_kernel,
        out_shape=jax.ShapeDtypeStruct(tokens.shape, BF16),
        in_specs=[hbm] + [vmem] * 4 + [hbm] * 6 + [vmem],
        out_specs=vmem,
        scratch_shapes=[
            pltpu.VMEM((WIDTH, HIDDEN), BF16),
            pltpu.VMEM((HIDDEN, WIDTH), BF16),
            pltpu.VMEM((3, WIDTH, COLS), BF16),
            pltpu.VMEM((WIDTH, WIDTH), BF16),
            pltpu.VMEM((4, ROWS, WIDTH), BF16),
            pltpu.VMEM((4, ROWS, WIDTH), BF16),
            pltpu.VMEM((8, ROWS, WIDTH), F32),
            pltpu.VMEM((4 * ROWS, HIDDEN), BF16),
            pltpu.VMEM((4 * ROWS, WIDTH), BF16),
            pltpu.VMEM((4, ROWS, WIDTH), BF16),
            pltpu.VMEM((GROUP, ROWS, WIDTH), BF16),
            pltpu.VMEM((2, everyone, 128), BF16),
            pltpu.VMEM((4, everyone, 128), BF16),
            pltpu.VMEM((4, everyone, 128), BF16),
            pltpu.VMEM((everyone, COLS), BF16),
            pltpu.VMEM((4, ROWS, WIDTH), BF16),
            pltpu.VMEM((GROUP, 8, 128), jnp.int32),
            pltpu.VMEM((8, everyone), F32),
            pltpu.VMEM((everyone, 1), F32),
            dma((10,)),
            dma((4,)),
            dma((4,)),
            dma((GROUP,)),
            dma((GROUP,)),
            dma((8,)),
            dma((GROUP,)),
            dma((GROUP,)),
            dma((GROUP,)),
            dma((GROUP,)),
            dma((GROUP,)),
        ],
        compiler_params=pltpu.CompilerParams(
            collective_id=0, has_side_effects=True, vmem_limit_bytes=60 << 20
        ),
        name="space_time_block",
    )(
        tokens,
        conv_taps,
        norm_first.reshape(1, WIDTH),
        norm_second.reshape(1, WIDTH),
        norm_third.reshape(1, WIDTH),
        w_in,
        w_out,
        w_query,
        w_key,
        w_value,
        w_output,
        info,
    )


def solution(mesh):
    rows = P("tm", "agent", None)
    whole = P()
    return jax.shard_map(
        per_device,
        mesh=mesh,
        in_specs=(rows,) + (whole,) * 10 + (P("agent"), P("agent")),
        out_specs=rows,
        check_vma=False,
    )
```

time: 236 us -> 63.4 us (0.27)
  the two profiles are of different devices: /device:TPU:1 before, /device:TPU:25 now
where the time goes in v1:
time: 63.4 us; the launch traced here: 63.2 us
  Pallas kernels  59.9 us (94%)
  local copies, waits for them, and re-layouts  2.48 us (4%)
  other arithmetic  0.81 us (1%)
    pallas_call x1, Pallas kernels, per_device(): pl.pallas_call(block_kernel, out_shape=jax.ShapeDtypeStruct(tokens.shape,...  59.9 us
    unnamed x1, local copies, waits for them, and re-layouts  1.87 us

profile of v1, /device:TPU:25, one launch (start us, length us, event | category | flops | bytes accessed | tf_op | source)
XLA Modules:
  0.0 63.2 jit_solution(2505449030344903757)
XLA Ops:
  0.0 0.8 %add_bitcast_fusion = (s32[1,128]{1,0:T(1,128)S(1)}, s32[1,128]{1,0:T(1,128)S(1)}) fusion(s32[64]{0:T(128)} %param.24, s32[64]{0:T(128)} %param.25), kind=kLoop, calls=%fused_computation | loop fusion | flops 256 | bytes 1536 | tf_op jit(solution)/shard_map/stack | solution.py:440
  0.8 0.6 stack.8.info_own
  1.4 59.9 %space_time_block.1 = bf16[4,64,1024]{2,1,0:T(8,128)(2,1)} custom-call(bf16[4,64,1024]{2,1,0:T(8,128)(2,1)} %tokens.1, f32[5,1024]{1,0:T(8,128)} %taps.1, f32[1,1024]{1,0:T(1,128)} %bitcast.7, f32[1,1024]{1,0:T(1,128)} %bitcast.8, f32[1,1024]{1,0:T(1,128)} %bitcast.9, bf16[1024,3072]{1,0:T(8,128)(2,1)} %w_in.1, bf16[3072,1024]{1,0:T(8,128)(2,1)} %w_out.1, ...), custom_call_target="tpu_custom_call" | custom-call | tf_op jit(solution)/shard_map/space_time_block/pallas_call | solution.py:444
  61.3 1.9 %copy.15 = bf16[4,64,1024]{2,1,0:T(8,128)(2,1)} copy(bf16[4,64,1024]{2,1,0:T(8,128)(2,1)} %space_time_block.1) | data formatting | bytes 1048576

commit v2 on v1

v2 whole, which is shorter than its diff:
```python
import functools

import jax
import jax.numpy as jnp
from jax import lax
from jax.experimental import pallas as pl
from jax.experimental.pallas import tpu as pltpu
from jax.sharding import PartitionSpec as P

EPS = 1e-05
HEADS = 16
MESH = pl.DeviceIdType.MESH
F32, BF16 = jnp.float32, jnp.bfloat16
GROUP = 16
ROWS = 64
WIDTH = 1024
HIDDEN = 3072
COLS = 256
FF_TILE = 1024
PIECES = 2
PIECE = ROWS // PIECES
SPAN = GROUP * PIECE
QUERIES = 256
HOMES = QUERIES // PIECE
SENDS = ((0, 1), (1, 0), (3, 0), (1, 1), (3, 1), (2, 0), (2, 1))


def remote(src, dst, send, recv, tm, agent):
    return pltpu.make_async_remote_copy(
        src_ref=src,
        dst_ref=dst,
        send_sem=send,
        recv_sem=recv,
        device_id=(tm, agent),
        device_id_type=MESH,
    )


def normed(rows, gain):
    scale = lax.rsqrt(jnp.mean(rows * rows, axis=-1, keepdims=True) + EPS)
    return rows * scale * gain


def block_kernel(
    tokens,
    taps,
    gain_first,
    gain_second,
    gain_third,
    w_in,
    w_out,
    w_query,
    w_key,
    w_value,
    w_output,
    order_own,
    present_own,
    result,
    win_v,
    wout_v,
    wqkv_v,
    wo_v,
    tok_v,
    prev_v,
    norm_v,
    inner_v,
    hid_v,
    second_v,
    mine_v,
    gath_v,
    query_v,
    key_v,
    value_v,
    att_v,
    back_v,
    info_v,
    okey_v,
    oquery_v,
    keep_v,
    local_sem,
    keep_sem,
    here_sem,
    shift_send,
    shift_recv,
    info_send,
    info_recv,
    ex_send,
    ex_recv,
    rel_send,
    rel_recv,
    ret_send,
    ret_recv,
):
    tm, me = lax.axis_index("tm"), lax.axis_index("agent")
    n_tm = lax.axis_size("tm")
    z, x, core = me // 4, lax.rem(me // 2, 2), lax.rem(me, 2)
    group = lax.rem(me, 4)
    sibling = me + 1 - 2 * core
    after, before = lax.rem(tm + 1, n_tm), lax.rem(tm + n_tm - 1, n_tm)

    cols = pl.ds(pl.multiple_of(group * COLS, COLS), COLS)
    loads = [
        pltpu.make_async_copy(tokens, tok_v, local_sem.at[0]),
        pltpu.make_async_copy(w_in, win_v, local_sem.at[1]),
        pltpu.make_async_copy(w_out, wout_v, local_sem.at[2]),
        pltpu.make_async_copy(w_query.at[:, cols], wqkv_v.at[0], local_sem.at[3]),
        pltpu.make_async_copy(w_key.at[:, cols], wqkv_v.at[1], local_sem.at[4]),
        pltpu.make_async_copy(w_value.at[:, cols], wqkv_v.at[2], local_sem.at[5]),
        pltpu.make_async_copy(w_output, wo_v, local_sem.at[6]),
    ]
    for load in loads:
        load.start()

    barrier = pltpu.get_barrier_semaphore()

    def greet(d, carry):
        pl.semaphore_signal(
            barrier, inc=1, device_id=(tm, lax.rem(me + d, GROUP)), device_id_type=MESH
        )
        return carry

    pl.semaphore_signal(barrier, inc=1, device_id=(before, me), device_id_type=MESH)
    pl.semaphore_signal(barrier, inc=1, device_id=(after, me), device_id_type=MESH)
    lax.fori_loop(1, GROUP, greet, 0)

    band = lax.rem(lax.broadcasted_iota(jnp.int32, (1, 128), 1) // PIECE, PIECES)
    info_v[me] = jnp.zeros((8, 128), jnp.int32)
    for number, source in enumerate((order_own, present_own)):
        info_v[me, 0:1, 0:ROWS] = source[...]
        once = info_v[me, 0:1, :]
        row = once + pltpu.roll(once, ROWS, 1)
        turned = [row] + [pltpu.roll(row, PIECE * i, 1) for i in range(1, PIECES)]
        for piece in range(PIECES):
            picked = row
            for i in range(1, PIECES):
                picked = jnp.where(lax.rem(band + PIECES - i, PIECES) == piece, turned[i], picked)
            keep_v[number * PIECES + piece : number * PIECES + piece + 1, :] = picked
    info_v[me, 0 : 2 * PIECES, :] = keep_v[0 : 2 * PIECES, :]

    pl.semaphore_wait(barrier, GROUP + 1)

    def shift(piece):
        rows = pl.ds(pl.multiple_of(piece * PIECE, PIECE), PIECE)
        return remote(
            tokens.at[:, rows, :],
            prev_v.at[:, rows, :],
            shift_send.at[piece],
            shift_recv.at[piece],
            after,
            me,
        )

    def info_copy(slot, peer):
        return remote(
            info_v.at[me], info_v.at[slot], info_send.at[peer], info_recv.at[slot], tm, peer
        )

    def tell(d, carry):
        info_copy(me, lax.rem(me + d, GROUP)).start()
        return carry

    lax.fori_loop(1, GROUP, tell, 0)

    @pl.when(tm < n_tm - 1)
    def _():
        for piece in range(PIECES):
            shift(piece).start()

    @pl.when(tm == 0)
    def _():
        def clear(i, carry):
            prev_v[i // 4, pl.ds(pl.multiple_of(lax.rem(i, 4) * 16, 16), 16), :] = jnp.zeros(
                (16, WIDTH), BF16
            )
            return carry

        lax.fori_loop(0, ROWS // 4, clear, 0)

    gain1, gain2, gain3 = gain_first[...], gain_second[...], gain_third[...]
    loads[0].wait()

    def feed(piece):
        rows = pl.ds(pl.multiple_of(piece * PIECE, PIECE), PIECE)
        for step in range(4):
            norm_v[4 + step] = normed(tok_v[step, rows].astype(F32), gain1)

        @pl.when(tm > 0)
        def _():
            shift(piece).wait_recv()

        for step in range(4):
            norm_v[step] = normed(prev_v[step, rows].astype(F32), gain1)
        firsts = []
        for step in range(4):
            mixed = taps[0:1, :] * norm_v[step + 4]
            for lag in range(1, 5):
                mixed = mixed + taps[lag : lag + 1, :] * norm_v[step + 4 - lag]
            firsts.append((tok_v[step, rows].astype(F32) + mixed).astype(BF16))
        first = jnp.concatenate(firsts, axis=0)
        second_v[piece] = first
        inner = normed(first.astype(F32), gain2).astype(BF16)
        inner_v[...] = inner

        def hidden(tile, carry):
            across = pl.ds(pl.multiple_of(tile * FF_TILE, FF_TILE), FF_TILE)
            pre = jnp.dot(inner_v[...], win_v[:, across], preferred_element_type=F32)
            act = 0.5 * pre * (1.0 + lax.erf(pre * 0.7071067811865476))
            hid_v[:, across] = act.astype(BF16)
            return carry

        lax.fori_loop(0, HIDDEN // FF_TILE, hidden, 0)
        ffn = jnp.dot(hid_v[...], wout_v[...], preferred_element_type=F32)
        second = (second_v[piece].astype(F32) + ffn).astype(BF16)
        second_v[piece] = second
        attn_in = normed(second.astype(F32), gain3).astype(BF16)
        for step in range(4):
            mine_v[piece, step] = attn_in[step * PIECE : (step + 1) * PIECE]

    def to_step(piece, turn, other):
        spot = piece * 8 + turn * 2 + other
        step = lax.rem(z + turn, 4)
        return remote(
            mine_v.at[piece, step],
            gath_v.at[piece, me],
            ex_send.at[spot],
            ex_recv.at[piece * GROUP + me],
            tm,
            step * 4 + 2 * ((1 - x) if other else x) + core,
        )

    def keep(piece):
        return pltpu.make_async_copy(
            mine_v.at[piece, z], gath_v.at[piece, me], keep_sem.at[piece]
        )

    def own_to_sibling(piece):
        return remote(
            mine_v.at[piece, z],
            gath_v.at[piece, me],
            rel_send.at[piece * GROUP + me],
            rel_recv.at[piece * GROUP + me],
            tm,
            sibling,
        )

    def spread(piece):
        @pl.when(tm == 0)
        def _():
            shift(piece).wait_send()

        keep(piece).start()
        own_to_sibling(piece).start()
        for turn, other in SENDS:
            to_step(piece, turn, other).start()


    def forward(piece, slot):
        return remote(
            gath_v.at[piece, slot],
            gath_v.at[piece, slot],
            rel_send.at[piece * GROUP + slot],
            rel_recv.at[piece * GROUP + slot],
            tm,
            sibling,
        )

    def others():
        return [
            lax.rem(z + 4 - turn, 4) * 4 + 2 * ((1 - x) if other else x) + core
            for turn, other in SENDS
        ]

    def relay(piece):
        for slot in others():
            remote(
                mine_v.at[piece, 0],
                gath_v.at[piece, slot],
                ex_send.at[0],
                ex_recv.at[piece * GROUP + slot],
                tm,
                slot,
            ).wait_recv()
            forward(piece, slot).start()

    lane = lax.broadcasted_iota(jnp.int32, (SPAN, 128), 1) < 64

    def project(piece):
        for slot in others() + [me]:
            forward(piece, slot + 1 - 2 * core).wait_recv()
        keep(piece).wait()
        rows = pl.ds(pl.multiple_of(piece * SPAN, SPAN), SPAN)
        source = gath_v[piece].reshape(SPAN, WIDTH)
        query = jnp.dot(source, wqkv_v[0], preferred_element_type=F32) * 0.125
        key = jnp.dot(source, wqkv_v[1], preferred_element_type=F32)
        value = jnp.dot(source, wqkv_v[2], preferred_element_type=F32)
        for pair in range(2):
            span = slice(pair * 128, pair * 128 + 128)
            query_v[pair, rows, :] = query[:, span].astype(BF16)
            key_v[2 * pair, rows, :] = jnp.where(lane, key[:, span], 0.0).astype(BF16)
            key_v[2 * pair + 1, rows, :] = jnp.where(lane, 0.0, key[:, span]).astype(BF16)
            value_v[2 * pair, rows, :] = jnp.where(lane, value[:, span], 1.0).astype(BF16)
            value_v[2 * pair + 1, rows, :] = jnp.where(lane, 1.0, value[:, span]).astype(BF16)

    def places():
        def heard(d, carry):
            peer = lax.rem(me + d, GROUP)
            info_copy(peer, peer).wait_recv()
            return carry

        lax.fori_loop(1, GROUP, heard, 0)
        now = tm * 4 + z
        eye = lax.broadcasted_iota(jnp.int32, (128, 128), 0) == lax.broadcasted_iota(
            jnp.int32, (128, 128), 1
        )
        part = lax.broadcasted_iota(jnp.int32, (1, 128), 1) // PIECE
        several = 128 // PIECE
        for piece in range(PIECES):
            for bunch in range(GROUP // several):
                place = info_v[bunch * several, piece : piece + 1]
                until = info_v[bunch * several, PIECES + piece : PIECES + piece + 1]
                for i in range(1, several):
                    tile = bunch * several + i
                    place = jnp.where(part == i, info_v[tile, piece : piece + 1], place)
                    until = jnp.where(
                        part == i, info_v[tile, PIECES + piece : PIECES + piece + 1], until
                    )
                place_f = place.astype(F32)
                start = piece * SPAN + bunch * 128
                okey_v[0:1, start : start + 128] = jnp.where(now < until, place_f, 1e9)
                oquery_v[start : start + 128, :] = jnp.sum(
                    jnp.where(eye, jnp.broadcast_to(place_f, (128, 128)), 0.0),
                    axis=1,
                    keepdims=True,
                )

    places()
    for load in loads[1:6]:
        load.wait()

    def produce(piece, carry):
        feed(piece)
        spread(piece)
        return carry

    def consume(piece, carry):
        relay(piece)
        project(piece)
        return carry

    lax.fori_loop(0, PIECES, produce, 0)
    lax.fori_loop(0, PIECES, consume, 0)


    def give(piece, home):
        return (
            att_v.at[pl.ds(pl.multiple_of(piece * SPAN + home * PIECE, PIECE), PIECE), :],
            back_v.at[piece, group, z],
        )

    def give_far(piece, home):
        source, target = give(piece, home)
        return remote(
            source,
            target,
            ret_send.at[piece * GROUP + home],
            ret_recv.at[piece * GROUP + me],
            tm,
            home,
        )

    def give_here(piece):
        source, target = give(piece, me)
        return pltpu.make_async_copy(source, target, here_sem.at[piece])

    half = lax.broadcasted_iota(jnp.int32, (QUERIES, 128), 1) < 64

    def attend(index, carry):
        start = pl.multiple_of(index * QUERIES, QUERIES)
        rows = pl.ds(start, QUERIES)
        row = lax.broadcasted_iota(jnp.int32, (QUERIES, GROUP * ROWS), 0) + start
        column = lax.broadcasted_iota(jnp.int32, (QUERIES, GROUP * ROWS), 1)
        visible = (okey_v[0:1, :] < oquery_v[rows, :]) | (row == column)
        bias = jnp.where(visible, 0.0, -1e30)
        for pair in range(2):
            query = query_v[pair, rows, :]
            parts = []
            for head in (2 * pair, 2 * pair + 1):
                scores = lax.dot_general(
                    query,
                    key_v[head],
                    (((1,), (1,)), ((), ())),
                    preferred_element_type=F32,
                )
                scores = scores + bias
                top = jnp.max(scores, axis=-1, keepdims=True)
                weights = jnp.exp(scores - top).astype(BF16)
                parts.append(jnp.dot(weights, value_v[head], preferred_element_type=F32))
            summed = jnp.where(half, parts[0], parts[1])
            total = pltpu.roll(jnp.where(half, parts[1], parts[0]), 64, 1)
            att_v[rows, pair * 128 : pair * 128 + 128] = (summed / total).astype(BF16)
        piece = start // SPAN
        first_home = lax.rem(start, SPAN) // PIECE
        for peer in range(HOMES):
            home = first_home + lax.rem(me + peer + 1, HOMES)

            @pl.when(home != me)
            def _(home=home):
                give_far(piece, home).start()

            @pl.when(home == me)
            def _():
                give_here(piece).start()

        return carry

    lax.fori_loop(0, GROUP * ROWS // QUERIES, attend, 0)

    loads[6].wait()
    def gather_home(piece, carry):
        give_here(piece).wait()

        def home_recv(d, carry):
            peer = lax.rem(me + d, GROUP)
            remote(
                att_v.at[pl.ds(0, PIECE), :],
                back_v.at[piece, lax.rem(peer, 4), peer // 4],
                ret_send.at[piece * GROUP + peer],
                ret_recv.at[piece * GROUP + peer],
                tm,
                peer,
            ).wait_recv()
            return carry

        lax.fori_loop(1, GROUP, home_recv, 0)
        attended = jnp.concatenate(
            [back_v[piece, heads].reshape(4 * PIECE, COLS) for heads in range(4)], axis=1
        )
        projected = jnp.dot(attended, wo_v[...], preferred_element_type=F32)
        done = (second_v[piece].astype(F32) + projected).astype(BF16)
        for step in range(4):
            result[step, pl.ds(pl.multiple_of(piece * PIECE, PIECE), PIECE), :] = done[
                step * PIECE : (step + 1) * PIECE
            ]
        return carry

    lax.fori_loop(0, PIECES, gather_home, 0)

    @pl.when((tm > 0) & (tm < n_tm - 1))
    def _():
        for piece in range(PIECES):
            shift(piece).wait_send()

    def drained(d, carry):
        peer = lax.rem(me + d, GROUP)
        info_copy(me, peer).wait_send()
        for piece in range(PIECES):
            give_far(piece, peer).wait_send()
        return carry

    lax.fori_loop(1, GROUP, drained, 0)
    for piece in range(PIECES):
        for turn, other in SENDS:
            to_step(piece, turn, other).wait_send()
        for slot in others() + [me]:
            forward(piece, slot).wait_send()


def per_device(
    tokens,
    conv_taps,
    norm_first,
    norm_second,
    norm_third,
    w_in,
    w_out,
    w_query,
    w_key,
    w_value,
    w_output,
    agent_order,
    present_steps,
):
    vmem, hbm = pl.BlockSpec(memory_space=pltpu.VMEM), pl.BlockSpec(memory_space=pl.ANY)
    dma = pltpu.SemaphoreType.DMA
    everyone = GROUP * ROWS
    return pl.pallas_call(
        block_kernel,
        out_shape=pltpu.VMEM(tokens.shape, BF16),
        in_specs=[hbm] + [vmem] * 4 + [hbm] * 6 + [vmem] * 2,
        out_specs=vmem,
        scratch_shapes=[
            pltpu.VMEM((WIDTH, HIDDEN), BF16),
            pltpu.VMEM((HIDDEN, WIDTH), BF16),
            pltpu.VMEM((3, WIDTH, COLS), BF16),
            pltpu.VMEM((WIDTH, WIDTH), BF16),
            pltpu.VMEM((4, ROWS, WIDTH), BF16),
            pltpu.VMEM((4, ROWS, WIDTH), BF16),
            pltpu.VMEM((8, PIECE, WIDTH), F32),
            pltpu.VMEM((4 * PIECE, WIDTH), BF16),
            pltpu.VMEM((4 * PIECE, HIDDEN), BF16),
            pltpu.VMEM((PIECES, 4 * PIECE, WIDTH), BF16),
            pltpu.VMEM((PIECES, 4, PIECE, WIDTH), BF16),
            pltpu.VMEM((PIECES, GROUP, PIECE, WIDTH), BF16),
            pltpu.VMEM((2, everyone, 128), BF16),
            pltpu.VMEM((4, everyone, 128), BF16),
            pltpu.VMEM((4, everyone, 128), BF16),
            pltpu.VMEM((everyone, COLS), BF16),
            pltpu.VMEM((PIECES, 4, 4, PIECE, COLS), BF16),
            pltpu.VMEM((GROUP, 8, 128), jnp.int32),
            pltpu.VMEM((8, everyone), F32),
            pltpu.VMEM((everyone, 1), F32),
            pltpu.VMEM((8, 128), jnp.int32),
            dma((7,)),
            dma((PIECES,)),
            dma((PIECES,)),
            dma((PIECES,)),
            dma((PIECES,)),
            dma((GROUP,)),
            dma((GROUP,)),
            dma((PIECES * 8,)),
            dma((PIECES * GROUP,)),
            dma((PIECES * GROUP,)),
            dma((PIECES * GROUP,)),
            dma((PIECES * GROUP,)),
            dma((PIECES * GROUP,)),
        ],
        compiler_params=pltpu.CompilerParams(
            collective_id=0, has_side_effects=True, vmem_limit_bytes=60 << 20
        ),
        name="space_time_block",
    )(
        tokens,
        conv_taps,
        norm_first.reshape(1, WIDTH),
        norm_second.reshape(1, WIDTH),
        norm_third.reshape(1, WIDTH),
        w_in,
        w_out,
        w_query,
        w_key,
        w_value,
        w_output,
        agent_order.reshape(1, ROWS),
        present_steps.reshape(1, ROWS),
    )


def solution(mesh):
    rows = P("tm", "agent", None)
    whole = P()
    return jax.shard_map(
        per_device,
        mesh=mesh,
        in_specs=(rows,) + (whole,) * 10 + (P("agent"), P("agent")),
        out_specs=rows,
        check_vma=False,
    )
```

time: 63.4 us -> 52.2 us (0.82)
  the two profiles are of different devices: /device:TPU:25 before, /device:TPU:1 now
where the time goes in v2:
time: 52.2 us; the launch traced here: 52.1 us
  Pallas kernels  51.3 us (98%)
  local copies, waits for them, and re-layouts  0.8 us (2%)
    pallas_call x1, Pallas kernels, per_device(): pl.pallas_call(block_kernel, out_shape=pltpu.VMEM(tokens.shape, BF16), in...  51.3 us

profile of v2, /device:TPU:1, one launch (start us, length us, event | category | flops | bytes accessed | tf_op | source)
XLA Modules:
  0.0 52.1 jit_solution(331229924760735897)
XLA Ops:
  0.0 51.3 %space_time_block.1 = bf16[4,64,1024]{2,1,0:T(8,128)(2,1)S(1)} custom-call(bf16[4,64,1024]{2,1,0:T(8,128)(2,1)} %tokens.1, f32[5,1024]{1,0:T(8,128)} %taps.1, f32[1,1024]{1,0:T(1,128)} %bitcast.5, f32[1,1024]{1,0:T(1,128)} %bitcast.6, f32[1,1024]{1,0:T(1,128)} %bitcast.7, bf16[1024,3072]{1,0:T(8,128)(2,1)} %w_in.1, bf16[3072,1024]{1,0:T(8,128)(2,1)} %w_out.1, ...), custom_call_target="tpu_custom_call" | custom-call | tf_op jit(solution)/shard_map/space_time_block/pallas_call | solution.py:486
  51.3 0.8 %copy.15 = bf16[4,64,1024]{2,1,0:T(8,128)(2,1)} copy(bf16[4,64,1024]{2,1,0:T(8,128)(2,1)S(1)} %space_time_block.1) | data formatting | bytes 1048576

commit v3 on v2

--- a/solution.py
+++ b/solution.py
@@ -77,6 +77,8 @@
     okey_v,
     oquery_v,
     keep_v,
+    top_v,
+    part_v,
     local_sem,
     keep_sem,
     here_sem,
@@ -119,8 +121,10 @@
         )
         return carry
 
-    pl.semaphore_signal(barrier, inc=1, device_id=(before, me), device_id_type=MESH)
-    pl.semaphore_signal(barrier, inc=1, device_id=(after, me), device_id_type=MESH)
+    @pl.when(tm > 0)
+    def _():
+        pl.semaphore_signal(barrier, inc=1, device_id=(before, me), device_id_type=MESH)
+
     lax.fori_loop(1, GROUP, greet, 0)
 
     band = lax.rem(lax.broadcasted_iota(jnp.int32, (1, 128), 1) // PIECE, PIECES)
@@ -137,7 +141,14 @@
             keep_v[number * PIECES + piece : number * PIECES + piece + 1, :] = picked
     info_v[me, 0 : 2 * PIECES, :] = keep_v[0 : 2 * PIECES, :]
 
-    pl.semaphore_wait(barrier, GROUP + 1)
+    @pl.when(tm < n_tm - 1)
+    def _():
+        pl.semaphore_wait(barrier, GROUP)
+
+    @pl.when(tm == n_tm - 1)
+    def _():
+        pl.semaphore_wait(barrier, GROUP - 1)
+
 
     def shift(piece):
         rows = pl.ds(pl.multiple_of(piece * PIECE, PIECE), PIECE)
@@ -342,13 +353,7 @@
         spread(piece)
         return carry
 
-    def consume(piece, carry):
-        relay(piece)
-        project(piece)
-        return carry
-
     lax.fori_loop(0, PIECES, produce, 0)
-    lax.fori_loop(0, PIECES, consume, 0)
 
 
     def give(piece, home):
@@ -372,48 +377,106 @@
         source, target = give(piece, me)
         return pltpu.make_async_copy(source, target, here_sem.at[piece])
 
-    half = lax.broadcasted_iota(jnp.int32, (QUERIES, 128), 1) < 64
-
-    def attend(index, carry):
-        start = pl.multiple_of(index * QUERIES, QUERIES)
-        rows = pl.ds(start, QUERIES)
-        row = lax.broadcasted_iota(jnp.int32, (QUERIES, GROUP * ROWS), 0) + start
-        column = lax.broadcasted_iota(jnp.int32, (QUERIES, GROUP * ROWS), 1)
-        visible = (okey_v[0:1, :] < oquery_v[rows, :]) | (row == column)
+    def heads(start, count, keys, combine):
+        rows = pl.ds(start, count)
+        width = keys.stop - keys.start
+        row = lax.broadcasted_iota(jnp.int32, (count, width), 0) + start
+        column = lax.broadcasted_iota(jnp.int32, (count, width), 1) + keys.start
+        visible = (okey_v[0:1, keys] < oquery_v[rows, :]) | (row == column)
         bias = jnp.where(visible, 0.0, -1e30)
+
+        def score(head):
+            return lax.dot_general(
+                query_v[head // 2, rows, :],
+                key_v[head, keys, :],
+                (((1,), (1,)), ((), ())),
+                preferred_element_type=F32,
+            )
+
+        def weigh(head, scores):
+            scores = scores + bias
+            top = jnp.max(scores, axis=-1, keepdims=True)
+            if combine:
+                top = jnp.maximum(top, top_v[head, rows, :])
+            return top, jnp.exp(scores - top).astype(BF16)
+
+        def total(head, top, weights):
+            part = jnp.dot(weights, value_v[head, keys, :], preferred_element_type=F32)
+            if combine:
+                part = part + part_v[head, rows, :] * jnp.exp(top_v[head, rows, :] - top)
+            return part
+
+        tops, parts = [], []
+        ahead = score(0)
+        behind = None
+        for head in range(4):
+            scores = ahead
+            if head < 3:
+                ahead = score(head + 1)
+            top, weights = weigh(head, scores)
+            if behind is not None:
+                parts.append(total(head - 1, *behind))
+            behind = (top, weights)
+            tops.append(top)
+        parts.append(total(3, *behind))
+        return tops, parts
+
+    def store(start, count, parts):
+        half = lax.broadcasted_iota(jnp.int32, (count, 128), 1) < 64
         for pair in range(2):
-            query = query_v[pair, rows, :]
-            parts = []
-            for head in (2 * pair, 2 * pair + 1):
-                scores = lax.dot_general(
-                    query,
-                    key_v[head],
-                    (((1,), (1,)), ((), ())),
-                    preferred_element_type=F32,
-                )
-                scores = scores + bias
-                top = jnp.max(scores, axis=-1, keepdims=True)
-                weights = jnp.exp(scores - top).astype(BF16)
-                parts.append(jnp.dot(weights, value_v[head], preferred_element_type=F32))
-            summed = jnp.where(half, parts[0], parts[1])
-            total = pltpu.roll(jnp.where(half, parts[1], parts[0]), 64, 1)
-            att_v[rows, pair * 128 : pair * 128 + 128] = (summed / total).astype(BF16)
-        piece = start // SPAN
-        first_home = lax.rem(start, SPAN) // PIECE
-        for peer in range(HOMES):
-            home = first_home + lax.rem(me + peer + 1, HOMES)
+            even, odd = parts[2 * pair : 2 * pair + 2]
+            summed = jnp.where(half, even, odd)
+            over = pltpu.roll(jnp.where(half, odd, even), 64, 1)
+            att_v[pl.ds(start, count), pair * 128 : pair * 128 + 128] = (summed / over).astype(BF16)
+
+    def send_home(piece, first_home, count):
+        def one(peer, carry):
+            home = first_home + lax.rem(me + peer + 1, count)
 
             @pl.when(home != me)
-            def _(home=home):
+            def _():
                 give_far(piece, home).start()
 
             @pl.when(home == me)
             def _():
                 give_here(piece).start()
 
-        return carry
-
-    lax.fori_loop(0, GROUP * ROWS // QUERIES, attend, 0)
+            return carry
+
+        lax.fori_loop(0, count, one, 0)
+
+    relay(0)
+    project(0)
+
+    def early(index, carry):
+        start = pl.multiple_of(index * QUERIES, QUERIES)
+        tops, parts = heads(start, QUERIES, slice(0, SPAN), False)
+        for head in range(4):
+            top_v[head, pl.ds(start, QUERIES), :] = tops[head]
+            part_v[head, pl.ds(start, QUERIES), :] = parts[head]
+        return carry
+
+    lax.fori_loop(0, SPAN // QUERIES, early, 0)
+    relay(1)
+    project(1)
+
+    def late(index, carry):
+        start = pl.multiple_of(index * QUERIES, QUERIES)
+        tops, parts = heads(start, QUERIES, slice(SPAN, 2 * SPAN), True)
+        store(start, QUERIES, parts)
+        send_home(0, index * HOMES, HOMES)
+        return carry
+
+    lax.fori_loop(0, SPAN // QUERIES, late, 0)
+
+    def attend(index, carry):
+        start = pl.multiple_of(SPAN + index * QUERIES, QUERIES)
+        tops, parts = heads(start, QUERIES, slice(0, 2 * SPAN), False)
+        store(start, QUERIES, parts)
+        send_home(1, index * HOMES, HOMES)
+        return carry
+
+    lax.fori_loop(0, SPAN // QUERIES, attend, 0)
 
     loads[6].wait()
     def gather_home(piece, carry):
@@ -433,7 +496,7 @@
 
         lax.fori_loop(1, GROUP, home_recv, 0)
         attended = jnp.concatenate(
-            [back_v[piece, heads].reshape(4 * PIECE, COLS) for heads in range(4)], axis=1
+            [back_v[piece, quarter].reshape(4 * PIECE, COLS) for quarter in range(4)], axis=1
         )
         projected = jnp.dot(attended, wo_v[...], preferred_element_type=F32)
         done = (second_v[piece].astype(F32) + projected).astype(BF16)
@@ -510,6 +573,8 @@
             pltpu.VMEM((8, everyone), F32),
             pltpu.VMEM((everyone, 1), F32),
             pltpu.VMEM((8, 128), jnp.int32),
+            pltpu.VMEM((4, SPAN, 1), F32),
+            pltpu.VMEM((4, SPAN, 128), F32),
             dma((7,)),
             dma((PIECES,)),
             dma((PIECES,)),

time: 52.2 us -> 49.1 us (0.941)
  Pallas kernels: 51.3 us -> 48.1 us
    pallas_call x1, Pallas kernels: 51.3 us -> 48.1 us  [per_device(): pl.pallas_call(block_kernel, out_shape=pltpu.VMEM(tokens.shape, BF16), in...]
where the time goes in v3:
time: 49.1 us; the launch traced here: 48.9 us
  Pallas kernels  48.1 us (98%)
  local copies, waits for them, and re-layouts  0.8 us (2%)
    pallas_call x1, Pallas kernels, per_device(): pl.pallas_call(block_kernel, out_shape=pltpu.VMEM(tokens.shape, BF16), in...  48.1 us

profile of v3, /device:TPU:1, one launch (start us, length us, event | category | flops | bytes accessed | tf_op | source)
XLA Modules:
  0.0 48.9 jit_solution(10605214117710250721)
XLA Ops:
  0.0 48.1 %space_time_block.1 = bf16[4,64,1024]{2,1,0:T(8,128)(2,1)S(1)} custom-call(bf16[4,64,1024]{2,1,0:T(8,128)(2,1)} %tokens.1, f32[5,1024]{1,0:T(8,128)} %taps.1, f32[1,1024]{1,0:T(1,128)} %bitcast.5, f32[1,1024]{1,0:T(1,128)} %bitcast.6, f32[1,1024]{1,0:T(1,128)} %bitcast.7, bf16[1024,3072]{1,0:T(8,128)(2,1)} %w_in.1, bf16[3072,1024]{1,0:T(8,128)(2,1)} %w_out.1, ...), custom_call_target="tpu_custom_call" | custom-call | tf_op jit(solution)/shard_map/space_time_block/pallas_call | solution.py:549
  48.1 0.8 %copy.15 = bf16[4,64,1024]{2,1,0:T(8,128)(2,1)} copy(bf16[4,64,1024]{2,1,0:T(8,128)(2,1)S(1)} %space_time_block.1) | data formatting | bytes 1048576

commit v4 on v3

--- a/solution.py
+++ b/solution.py
@@ -43,7 +43,7 @@
 
 def block_kernel(
     tokens,
-    taps,
+    taps_in,
     gain_first,
     gain_second,
     gain_third,
@@ -56,6 +56,9 @@
     order_own,
     present_own,
     result,
+    taps,
+    gains_v,
+    own_v,
     win_v,
     wout_v,
     wqkv_v,
@@ -79,6 +82,7 @@
     keep_v,
     top_v,
     part_v,
+    small_sem,
     local_sem,
     keep_sem,
     here_sem,
@@ -101,6 +105,12 @@
     after, before = lax.rem(tm + 1, n_tm), lax.rem(tm + n_tm - 1, n_tm)
 
     cols = pl.ds(pl.multiple_of(group * COLS, COLS), COLS)
+    small = [
+        pltpu.make_async_copy(taps_in, taps, small_sem.at[0]),
+        pltpu.make_async_copy(gain_first, gains_v.at[0:1], small_sem.at[1]),
+        pltpu.make_async_copy(gain_second, gains_v.at[1:2], small_sem.at[2]),
+        pltpu.make_async_copy(gain_third, gains_v.at[2:3], small_sem.at[3]),
+    ]
     loads = [
         pltpu.make_async_copy(tokens, tok_v, local_sem.at[0]),
         pltpu.make_async_copy(w_in, win_v, local_sem.at[1]),
@@ -110,9 +120,6 @@
         pltpu.make_async_copy(w_value.at[:, cols], wqkv_v.at[2], local_sem.at[5]),
         pltpu.make_async_copy(w_output, wo_v, local_sem.at[6]),
     ]
-    for load in loads:
-        load.start()
-
     barrier = pltpu.get_barrier_semaphore()
 
     def greet(d, carry):
@@ -126,12 +133,15 @@
         pl.semaphore_signal(barrier, inc=1, device_id=(before, me), device_id_type=MESH)
 
     lax.fori_loop(1, GROUP, greet, 0)
+    own_v[...] = jnp.zeros_like(own_v)
+    for load in small + loads:
+        load.start()
+    own_v[0:1, 0:ROWS] = order_own[...]
+    own_v[1:2, 0:ROWS] = present_own[...]
 
     band = lax.rem(lax.broadcasted_iota(jnp.int32, (1, 128), 1) // PIECE, PIECES)
-    info_v[me] = jnp.zeros((8, 128), jnp.int32)
-    for number, source in enumerate((order_own, present_own)):
-        info_v[me, 0:1, 0:ROWS] = source[...]
-        once = info_v[me, 0:1, :]
+    for number in range(2):
+        once = own_v[number : number + 1, :]
         row = once + pltpu.roll(once, ROWS, 1)
         turned = [row] + [pltpu.roll(row, PIECE * i, 1) for i in range(1, PIECES)]
         for piece in range(PIECES):
@@ -139,7 +149,7 @@
             for i in range(1, PIECES):
                 picked = jnp.where(lax.rem(band + PIECES - i, PIECES) == piece, turned[i], picked)
             keep_v[number * PIECES + piece : number * PIECES + piece + 1, :] = picked
-    info_v[me, 0 : 2 * PIECES, :] = keep_v[0 : 2 * PIECES, :]
+    info_v[me] = keep_v[...]
 
     @pl.when(tm < n_tm - 1)
     def _():
@@ -163,7 +173,7 @@
 
     def info_copy(slot, peer):
         return remote(
-            info_v.at[me], info_v.at[slot], info_send.at[peer], info_recv.at[slot], tm, peer
+            info_v.at[me], info_v.at[slot], info_send.at[0], info_recv.at[0], tm, peer
         )
 
     def tell(d, carry):
@@ -187,7 +197,9 @@
 
         lax.fori_loop(0, ROWS // 4, clear, 0)
 
-    gain1, gain2, gain3 = gain_first[...], gain_second[...], gain_third[...]
+    for load in small:
+        load.wait()
+    gain1, gain2, gain3 = gains_v[0:1], gains_v[1:2], gains_v[2:3]
     loads[0].wait()
 
     def feed(piece):
@@ -228,12 +240,11 @@
             mine_v[piece, step] = attn_in[step * PIECE : (step + 1) * PIECE]
 
     def to_step(piece, turn, other):
-        spot = piece * 8 + turn * 2 + other
         step = lax.rem(z + turn, 4)
         return remote(
             mine_v.at[piece, step],
             gath_v.at[piece, me],
-            ex_send.at[spot],
+            ex_send.at[piece],
             ex_recv.at[piece * GROUP + me],
             tm,
             step * 4 + 2 * ((1 - x) if other else x) + core,
@@ -248,8 +259,8 @@
         return remote(
             mine_v.at[piece, z],
             gath_v.at[piece, me],
-            rel_send.at[piece * GROUP + me],
-            rel_recv.at[piece * GROUP + me],
+            rel_send.at[piece],
+            rel_recv.at[piece],
             tm,
             sibling,
         )
@@ -269,8 +280,8 @@
         return remote(
             gath_v.at[piece, slot],
             gath_v.at[piece, slot],
-            rel_send.at[piece * GROUP + slot],
-            rel_recv.at[piece * GROUP + slot],
+            rel_send.at[piece],
+            rel_recv.at[piece],
             tm,
             sibling,
         )
@@ -293,11 +304,18 @@
             ).wait_recv()
             forward(piece, slot).start()
 
+    def relayed(piece):
+        eight = gath_v.at[piece, pl.ds(0, GROUP // 2)]
+        return remote(eight, eight, rel_send.at[piece], rel_recv.at[piece], tm, sibling)
+
+    def spreaded(piece):
+        seven = gath_v.at[piece, pl.ds(0, len(SENDS))]
+        return remote(seven, seven, ex_send.at[piece], rel_recv.at[piece], tm, sibling)
+
     lane = lax.broadcasted_iota(jnp.int32, (SPAN, 128), 1) < 64
 
     def project(piece):
-        for slot in others() + [me]:
-            forward(piece, slot + 1 - 2 * core).wait_recv()
+        relayed(piece).wait_recv()
         keep(piece).wait()
         rows = pl.ds(pl.multiple_of(piece * SPAN, SPAN), SPAN)
         source = gath_v[piece].reshape(SPAN, WIDTH)
@@ -313,12 +331,10 @@
             value_v[2 * pair + 1, rows, :] = jnp.where(lane, 1.0, value[:, span]).astype(BF16)
 
     def places():
-        def heard(d, carry):
-            peer = lax.rem(me + d, GROUP)
-            info_copy(peer, peer).wait_recv()
-            return carry
-
-        lax.fori_loop(1, GROUP, heard, 0)
+        told = info_v.at[pl.ds(0, GROUP - 1)]
+        both = remote(told, told, info_send.at[0], info_recv.at[0], tm, sibling)
+        both.wait_recv()
+        both.wait_send()
         now = tm * 4 + z
         eye = lax.broadcasted_iota(jnp.int32, (128, 128), 0) == lax.broadcasted_iota(
             jnp.int32, (128, 128), 1
@@ -367,11 +383,15 @@
         return remote(
             source,
             target,
-            ret_send.at[piece * GROUP + home],
-            ret_recv.at[piece * GROUP + me],
+            ret_send.at[piece],
+            ret_recv.at[piece],
             tm,
             home,
         )
+
+    def returned(piece):
+        fifteen = att_v.at[pl.ds(0, (GROUP - 1) * PIECE), :]
+        return remote(fifteen, fifteen, ret_send.at[piece], ret_recv.at[piece], tm, sibling)
 
     def give_here(piece):
         source, target = give(piece, me)
@@ -460,6 +480,15 @@
     relay(1)
     project(1)
 
+    @pl.when((tm > 0) & (tm < n_tm - 1))
+    def _():
+        for piece in range(PIECES):
+            shift(piece).wait_send()
+
+    for piece in range(PIECES):
+        spreaded(piece).wait_send()
+        relayed(piece).wait_send()
+
     def late(index, carry):
         start = pl.multiple_of(index * QUERIES, QUERIES)
         tops, parts = heads(start, QUERIES, slice(SPAN, 2 * SPAN), True)
@@ -482,19 +511,8 @@
     def gather_home(piece, carry):
         give_here(piece).wait()
 
-        def home_recv(d, carry):
-            peer = lax.rem(me + d, GROUP)
-            remote(
-                att_v.at[pl.ds(0, PIECE), :],
-                back_v.at[piece, lax.rem(peer, 4), peer // 4],
-                ret_send.at[piece * GROUP + peer],
-                ret_recv.at[piece * GROUP + peer],
-                tm,
-                peer,
-            ).wait_recv()
-            return carry
-
-        lax.fori_loop(1, GROUP, home_recv, 0)
+        returned(piece).wait_recv()
+        returned(piece).wait_send()
         attended = jnp.concatenate(
             [back_v[piece, quarter].reshape(4 * PIECE, COLS) for quarter in range(4)], axis=1
         )
@@ -507,25 +525,6 @@
         return carry
 
     lax.fori_loop(0, PIECES, gather_home, 0)
-
-    @pl.when((tm > 0) & (tm < n_tm - 1))
-    def _():
-        for piece in range(PIECES):
-            shift(piece).wait_send()
-
-    def drained(d, carry):
-        peer = lax.rem(me + d, GROUP)
-        info_copy(me, peer).wait_send()
-        for piece in range(PIECES):
-            give_far(piece, peer).wait_send()
-        return carry
-
-    lax.fori_loop(1, GROUP, drained, 0)
-    for piece in range(PIECES):
-        for turn, other in SENDS:
-            to_step(piece, turn, other).wait_send()
-        for slot in others() + [me]:
-            forward(piece, slot).wait_send()
 
 
 def per_device(
@@ -549,9 +548,12 @@
     return pl.pallas_call(
         block_kernel,
         out_shape=pltpu.VMEM(tokens.shape, BF16),
-        in_specs=[hbm] + [vmem] * 4 + [hbm] * 6 + [vmem] * 2,
+        in_specs=[hbm] * 11 + [vmem] * 2,
         out_specs=vmem,
         scratch_shapes=[
+            pltpu.VMEM((5, WIDTH), F32),
+            pltpu.VMEM((3, WIDTH), F32),
+            pltpu.VMEM((8, 128), jnp.int32),
             pltpu.VMEM((WIDTH, HIDDEN), BF16),
             pltpu.VMEM((HIDDEN, WIDTH), BF16),
             pltpu.VMEM((3, WIDTH, COLS), BF16),
@@ -575,19 +577,20 @@
             pltpu.VMEM((8, 128), jnp.int32),
             pltpu.VMEM((4, SPAN, 1), F32),
             pltpu.VMEM((4, SPAN, 128), F32),
+            dma((4,)),
             dma((7,)),
             dma((PIECES,)),
             dma((PIECES,)),
             dma((PIECES,)),
             dma((PIECES,)),
-            dma((GROUP,)),
-            dma((GROUP,)),
-            dma((PIECES * 8,)),
+            dma((1,)),
+            dma((1,)),
+            dma((PIECES,)),
             dma((PIECES * GROUP,)),
-            dma((PIECES * GROUP,)),
-            dma((PIECES * GROUP,)),
-            dma((PIECES * GROUP,)),
-            dma((PIECES * GROUP,)),
+            dma((PIECES,)),
+            dma((PIECES,)),
+            dma((PIECES,)),
+            dma((PIECES,)),
         ],
         compiler_params=pltpu.CompilerParams(
             collective_id=0, has_side_effects=True, vmem_limit_bytes=60 << 20

time: 49.1 us -> 47.4 us (0.965)
  Pallas kernels: 48.1 us -> 46.5 us
    pallas_call x1, Pallas kernels: 48.1 us -> 46.5 us  [per_device(): pl.pallas_call(block_kernel, out_shape=pltpu.VMEM(tokens.shape, BF16), in...]
where the time goes in v4:
time: 47.4 us; the launch traced here: 47.3 us
  Pallas kernels  46.5 us (98%)
  local copies, waits for them, and re-layouts  0.8 us (2%)
    pallas_call x1, Pallas kernels, per_device(): pl.pallas_call(block_kernel, out_shape=pltpu.VMEM(tokens.shape, BF16), in...  46.5 us

profile of v4, /device:TPU:1, one launch (start us, length us, event | category | flops | bytes accessed | tf_op | source)
XLA Modules:
  0.0 47.3 jit_solution(1625126971993846708)
XLA Ops:
  0.0 46.5 %space_time_block.1 = bf16[4,64,1024]{2,1,0:T(8,128)(2,1)S(1)} custom-call(bf16[4,64,1024]{2,1,0:T(8,128)(2,1)} %tokens.1, f32[5,1024]{1,0:T(8,128)} %taps_in.1, f32[1,1024]{1,0:T(1,128)} %bitcast.5, f32[1,1024]{1,0:T(1,128)} %bitcast.6, f32[1,1024]{1,0:T(1,128)} %bitcast.7, bf16[1024,3072]{1,0:T(8,128)(2,1)} %w_in.1, bf16[3072,1024]{1,0:T(8,128)(2,1)} %w_out.1, ...), custom_call_target="tpu_custom_call" | custom-call | tf_op jit(solution)/shard_map/space_time_block/pallas_call | solution.py:548
  46.5 0.8 %copy.15 = bf16[4,64,1024]{2,1,0:T(8,128)(2,1)} copy(bf16[4,64,1024]{2,1,0:T(8,128)(2,1)S(1)} %space_time_block.1) | data formatting | bytes 1048576

commit v5 on v4

--- a/solution.py
+++ b/solution.py
@@ -22,7 +22,7 @@
 SPAN = GROUP * PIECE
 QUERIES = 256
 HOMES = QUERIES // PIECE
-SENDS = ((0, 1), (1, 0), (3, 0), (1, 1), (3, 1), (2, 0), (2, 1))
+SENDS = ((2, 1), (1, 1), (3, 1), (2, 0), (0, 1), (1, 0), (3, 0))
 
 
 def remote(src, dst, send, recv, tm, agent):

time: 47.4 us -> 46.9 us (0.989)
  Pallas kernels: 46.5 us -> 45.6 us
    pallas_call x1, Pallas kernels: 46.5 us -> 45.6 us  [per_device(): pl.pallas_call(block_kernel, out_shape=pltpu.VMEM(tokens.shape, BF16), in...]
where the time goes in v5:
time: 46.9 us; the launch traced here: 46.4 us
  Pallas kernels  45.6 us (97%)
  local copies, waits for them, and re-layouts  0.8 us (2%)
    pallas_call x1, Pallas kernels, per_device(): pl.pallas_call(block_kernel, out_shape=pltpu.VMEM(tokens.shape, BF16), in...  45.6 us

profile of v5, /device:TPU:1, one launch (start us, length us, event | category | flops | bytes accessed | tf_op | source)
XLA Modules:
  0.0 46.4 jit_solution(14315566504733068690)
XLA Ops:
  0.0 45.6 %space_time_block.1 = bf16[4,64,1024]{2,1,0:T(8,128)(2,1)S(1)} custom-call(bf16[4,64,1024]{2,1,0:T(8,128)(2,1)} %tokens.1, f32[5,1024]{1,0:T(8,128)} %taps_in.1, f32[1,1024]{1,0:T(1,128)} %bitcast.5, f32[1,1024]{1,0:T(1,128)} %bitcast.6, f32[1,1024]{1,0:T(1,128)} %bitcast.7, bf16[1024,3072]{1,0:T(8,128)(2,1)} %w_in.1, bf16[3072,1024]{1,0:T(8,128)(2,1)} %w_out.1, ...), custom_call_target="tpu_custom_call" | custom-call | tf_op jit(solution)/shard_map/space_time_block/pallas_call | solution.py:548
  45.6 0.8 %copy.15 = bf16[4,64,1024]{2,1,0:T(8,128)(2,1)} copy(bf16[4,64,1024]{2,1,0:T(8,128)(2,1)S(1)} %space_time_block.1) | data formatting | bytes 1048576
